TPU v7x, 32 devices: a whole 2x2x4 slice. The times are simulated.
32 devices in a mesh: fsdp: 8 (over y, x, core), rep: 4 (over z).
Axes of the slice: x: 2, y: 2, z: 4, core: 2. Of those that a mesh axis runs over, the one named last changes fastest.
Arguments:
- inputs: bfloat16 [4, 1024, 4096], P('rep', 'fsdp'), may hold values from -6 to 6
- out_grad: bfloat16 [4, 1024, 512], P('rep', 'fsdp'), may hold values from -6 to 6
- weight: bfloat16 [4096, 512], P('fsdp'), may hold values from -6 to 6
- momentum: float32 [4, 512, 4096], P('rep', 'fsdp'), may hold values from -6 to 6
- band_index: int32 [128], replicated, may hold values from 0 to 511, as said below
Outputs:
- leftover: float32 [4, 512, 4096], P('rep', 'fsdp')
- new_weight: bfloat16 [4096, 512], P('fsdp')
- values: bfloat16 [4, 1024, 512], P('rep', 'fsdp')
Inputs may be any that keep to these rules, and one draw needn't show every extreme that they name: `band_index`: distinct entries below 512; 0 and 511 are always among them.
All inputs are finite; a program needn't handle non-finite values.
Results may differ from a plain program's by a relative error of at most 0.0049.
Values may be sent and summed in bfloat16 or wider, within the bound.
A program may use at most 64 MiB of HBM per device.

v0:
```python
import math

import jax
import jax.numpy as jnp
from jax import lax
from jax.sharding import PartitionSpec as P

MOMENTUM_DECAY = 0.9
LEARNING_RATE = 4.0


def dct_rows(band_index, length):
    positions = lax.iota(jnp.int32, length)
    phase_int = (2 * positions[None, :] + 1) * band_index[:, None] % (4 * length)
    angles = phase_int.astype(jnp.float32) * (math.pi / (2 * length))
    row_scale = jnp.where(band_index == 0, math.sqrt(1.0 / length), math.sqrt(2.0 / length)).astype(
        jnp.float32
    )
    return row_scale[:, None] * jnp.cos(angles)


def rebuild_rows(old_rows, update_rows):
    return (old_rows.astype(jnp.float32) - LEARNING_RATE * update_rows).astype(jnp.bfloat16)


def shards(inputs, out_grad, weight, momentum, band_index):
    tok_inputs = inputs[0]
    upstream = out_grad[0]
    own_rows = weight.shape[0]
    width_out = weight.shape[1]
    group_len = momentum.shape[2]
    scaling = 1.0 / math.sqrt(tok_inputs.shape[1])
    highest = lax.Precision.HIGHEST
    own_columns = lax.all_to_all(tok_inputs, "fsdp", split_axis=1, concat_axis=0, tiled=True)
    gradient = (
        lax.dot_general(
            own_columns,
            lax.all_gather(upstream, "fsdp", axis=0, tiled=True),
            (((0,), (0,)), ((), ())),
            preferred_element_type=jnp.float32,
        )
        * scaling
    )
    moment = MOMENTUM_DECAY * momentum[0] + gradient.reshape(-1, group_len)
    dct_basis = dct_rows(band_index, group_len)
    coeffs = jnp.dot(moment, dct_basis.T, precision=highest)
    leftover = (moment - jnp.dot(coeffs, dct_basis, precision=highest))[None]
    shared = lax.psum(coeffs, "rep") / lax.axis_size("rep")
    own_update = jnp.dot(shared, dct_basis, precision=highest).reshape(own_rows, width_out)
    new_weight = rebuild_rows(weight, own_update)
    running = jnp.dot(
        tok_inputs,
        lax.all_gather(new_weight, "fsdp", axis=0, tiled=True),
        preferred_element_type=jnp.float32,
    )
    values = (running * scaling).astype(jnp.bfloat16)[None]
    return (leftover, new_weight, values)


def solution(mesh):
    placed = (
        P("rep", "fsdp", None),
        P("rep", "fsdp", None),
        P("fsdp", None),
        P("rep", "fsdp", None),
        P(),
    )
    return jax.shard_map(
        shards,
        mesh=mesh,
        in_specs=placed,
        out_specs=(P("rep", "fsdp", None), P("fsdp", None), P("rep", "fsdp", None)),
        check_vma=False,
    )
```

profile of v0, /device:TPU:0, one launch (start us, length us, event | category | flops | bytes accessed | tf_op | source)
XLA Modules:
  0.0 127.6 jit_solution(9258728796929510348)
XLA Ops:
  7.2 0.0 all-gather.6.cloned.1.call-start
  7.2 0.7 all-gather.6.cloned.1.call-update
  7.9 0.0 copy-start.2
  7.9 2.3 %copy.10 = bf16[1,128,4096]{1,2,0:T(8,128)(2,1)} copy(bf16[1,128,4096]{2,1,0:T(8,128)(2,1)} %param.5) | data formatting | bytes 2097152 | tf_op args[0]
  10.2 5.2 %all-to-all-start = ((bf16[128,8,512]{0,2,1:T(8,128)(2,1)}), bf16[128,8,512]{0,2,1:T(8,128)(2,1)S(1)}, u32[]{:S(2)}, u32[]{:S(2)}) async-start(bf16[128,8,512]{0,2,1:T(8,128)(2,1)} %bitcast.1), calls=%async_computation | async-start | bytes 2097152 | tf_op jit(solution)/shard_map/all_to_all | solution.py:34
  15.4 0.0 all-gather.4.cloned.1.call-start
  15.4 0.0 copy-done.2
  15.5 16.7 %all-to-all-done = bf16[128,8,512]{0,2,1:T(8,128)(2,1)S(1)} async-done(((bf16[128,8,512]{0,2,1:T(8,128)(2,1)}), bf16[128,8,512]{0,2,1:T(8,128)(2,1)S(1)}, u32[]{:S(2)}, u32[]{:S(2)}) %all-to-all-start) | async-done | bytes 1048608 | tf_op jit(solution)/shard_map/all_to_all | solution.py:34
  32.1 0.5 copy.11
  32.6 6.3 %all-gather.6.cloned.1.call-done = bf16[1,1024,512]{2,1,0:T(8,128)(2,1)} async-done(((bf16[1,128,512]{2,1,0:T(8,128)(2,1)}), bf16[1,1024,512]{2,1,0:T(8,128)(2,1)}) %all-gather.6.cloned.1.call-update) | async-done | bytes 1048592 | tf_op jit(solution)/shard_map/all_gather | solution.py:38
  38.9 2.0 %convolution_multiply_fusion.1 = f32[512,512]{1,0:T(8,128)S(1)} fusion(bf16[1024,512]{1,0:T(8,128)(2,1)S(1)} %bitcast.24, bf16[1,1024,512]{2,1,0:T(8,128)(2,1)} %all-gather.6.cloned.1.call-done), kind=kOutput, calls=%fused_computation.13 | convolution fusion | flops 537133056 | bytes 3145728 | tf_op jit(solution)/shard_map/dot_general | solution.py:36
  40.9 0.2 reshape.27
  41.1 11.0 %fusion.12 = f32[64,128]{1,0:T(8,128)S(1)} fusion(s32[128]{0:T(128)S(1)} %copy-done.2, s32[4096]{0:T(1024)S(1)} %multiply_add_fusion, f32[128]{0:T(128)S(1)} %compare_select_fusion, f32[64,4096]{1,0:T(8,128)S(1)} %reshape.27, f32[1,64,4096]{2,1,0:T(8,128)} %param.8), kind=kOutput, calls=%fused_computation.21 | convolution fusion | flops 411041792 | bytes 2147328 | tf_op jit(solution)/shard_map/dot_general | solution.py:46
  52.1 19.2 %psum.7 = f32[64,128]{1,0:T(8,128)S(1)} all-reduce(f32[64,128]{1,0:T(8,128)S(1)} %fusion.12), channel_id=1, replica_groups=mesh['fsdp'=8,'rep'=4] {'rep'}, use_global_device_ids=true, to_apply=%region_0.1 | all-reduce | flops 8192 | bytes 65536 | tf_op jit(solution)/shard_map/psum | solution.py:48
  71.3 8.9 %convolution_multiply_fusion = f32[64,4096]{1,0:T(8,128)S(1)} fusion(s32[128]{0:T(128)S(1)} %copy-done.2, s32[4096]{0:T(1024)S(1)} %multiply_add_fusion, f32[128]{0:T(128)S(1)} %compare_select_fusion, f32[64,128]{1,0:T(8,128)S(1)} %psum.7), kind=kOutput, calls=%fused_computation | convolution fusion | flops 410787840 | bytes 1098752 | tf_op jit(solution)/shard_map/dot_general | solution.py:49
  80.2 0.2 mul.85
  80.4 0.0 copy-start.1
  80.4 2.1 %subtract_convert_fusion = bf16[512,512]{1,0:T(8,128)(2,1)} fusion(f32[512,512]{1,0:T(8,128)S(1)} %mul.85, bf16[512,512]{1,0:T(8,128)(2,1)} %param.7), kind=kLoop, calls=%fused_computation.20 | loop fusion | flops 786432 | bytes 2097152 | tf_op jit(solution)/shard_map/convert_element_type | solution.py:23
  82.5 0.0 all-gather.4.cloned.1.call-update
  82.5 0.0 copy-done.1
  82.5 0.0 copy-start
  82.5 10.2 %fusion = f32[1,64,4096]{2,1,0:T(8,128)} fusion(f32[64,128]{1,0:T(8,128)S(1)} %fusion.12, s32[128]{0:T(128)S(1)} %copy-done.2, s32[4096]{0:T(1024)S(1)} %multiply_add_fusion, f32[128]{0:T(128)S(1)} %compare_select_fusion, f32[64,4096]{1,0:T(8,128)S(1)} %reshape.27, f32[1,64,4096]{2,1,0:T(8,128)S(1)} %copy-done.1), kind=kOutput, calls=%fused_computation.2 | convolution fusion | flops 411303936 | bytes 3195904 | tf_op jit(solution)/shard_map/dot_general | solution.py:47
  92.8 23.7 %all-gather.4.cloned.1.call-done = bf16[4096,512]{1,0:T(8,128)(2,1)} async-done(((bf16[512,512]{1,0:T(8,128)(2,1)}), bf16[4096,512]{1,0:T(8,128)(2,1)}) %all-gather.4.cloned.1.call-update) | async-done | bytes 4194320 | tf_op jit(solution)/shard_map/all_gather | solution.py:53
  116.5 0.0 copy-done
  116.5 3.5 %fusion.7 = bf16[1,128,512]{1,2,0:T(8,128)(2,1)S(1)} fusion(bf16[4096,512]{1,0:T(8,128)(2,1)} %all-gather.4.cloned.1.call-done, bf16[1,128,4096]{2,1,0:T(8,128)(2,1)S(1)} %copy-done), kind=kOutput, calls=%fused_computation.16 | convolution fusion | flops 537001984 | bytes 5373952 | tf_op jit(solution)/shard_map/dot_general | solution.py:51
  120.0 0.8 copy.12
  (2 shorter events, 0.0 us)
Async XLA Ops:
  7.2 31.8 %all-gather.6.cloned.1.call-start = ((), (), s32[]{:S(2)}) async-start(), calls=%async_computation.2 | async-start | bytes 1179648 | tf_op jit(solution)/shard_map/all_gather | solution.py:38
  7.9 7.5 %copy-start.2 = (s32[128]{0:T(128)S(1)}, s32[128]{0:T(128)}, u32[]{:S(2)}) copy-start(s32[128]{0:T(128)} %param.9) | copy-start | bytes 1540
  10.2 21.9 %all-to-all-start = ((bf16[128,8,512]{0,2,1:T(8,128)(2,1)}), bf16[128,8,512]{0,2,1:T(8,128)(2,1)S(1)}, u32[]{:S(2)}, u32[]{:S(2)}) async-start(bf16[128,8,512]{0,2,1:T(8,128)(2,1)} %bitcast.1), calls=%async_computation | async-start | bytes 2097152 | tf_op jit(solution)/shard_map/all_to_all | solution.py:34
  15.4 101.1 %all-gather.4.cloned.1.call-start = ((), (), s32[]{:S(2)}) async-start(), calls=%async_computation.1 | async-start | bytes 4718592 | tf_op jit(solution)/shard_map/all_gather | solution.py:53
  80.4 2.1 %copy-start.1 = (f32[1,64,4096]{2,1,0:T(8,128)S(1)}, f32[1,64,4096]{2,1,0:T(8,128)}, u32[]{:S(2)}) copy-start(f32[1,64,4096]{2,1,0:T(8,128)} %param.8) | copy-start | bytes 3145732
  82.5 34.0 %copy-start = (bf16[1,128,4096]{2,1,0:T(8,128)(2,1)S(1)}, bf16[1,128,4096]{2,1,0:T(8,128)(2,1)}, u32[]{:S(2)}) copy-start(bf16[1,128,4096]{2,1,0:T(8,128)(2,1)} %param.5) | copy-start | bytes 3145732
Sparse Core Ops, SparseCore 0:
  9.9 29.0 all-gather.5
  82.6 33.8 all-gather.3
where the time goes:
time: 128 us
  waiting for transfers between devices  47.4 us (37%)
  matrix products  35.6 us (28%)
  blocking collectives  19.2 us (15%)
  between operations  14.1 us (11%)
  starting transfers between devices  5.27 us (4%)
  local copies, waits for them, and re-layouts  3.96 us (3%)
  other arithmetic  2.09 us (2%)
    all_gather x1, waiting for transfers between devices, shards(): lax.all_gather(new_weight, 'fsdp', axis=0, tiled=True)  23.7 us
    psum x1, blocking collectives, shards(): shared = lax.psum(coeffs, 'rep') / lax.axis_size('rep')  19.2 us
    all_to_all x1, waiting for transfers between devices, shards(): lax.all_to_all(tok_inputs, 'fsdp', split_axis=1, concat_axis=0, tiled=True)  16.7 us
    dot_general x1, matrix products, shards(): coeffs = jnp.dot(moment, dct_basis.T, precision=highest)  11 us
    dot_general x1, matrix products, shards(): leftover = (moment - jnp.dot(coeffs, dct_basis, precision=highest))[None]  10.2 us
    dot_general x1, matrix products, shards(): jnp.dot(shared, dct_basis, precision=highest).reshape(own_rows, width_out)  8.93 us
    all_gather x1, waiting for transfers between devices, shards(): lax.all_gather(upstream, 'fsdp', axis=0, tiled=True)  6.3 us
    all_to_all x1, starting transfers between devices, shards(): lax.all_to_all(tok_inputs, 'fsdp', split_axis=1, concat_axis=0, tiled=True)  5.2 us
  transfers between devices with their start and end apart: 3, of which 3 were waited for; matrix products, arithmetic and copies ran while one was open for 10% of the time, Pallas kernels for 0%

commit v1 on v0

--- a/solution.py
+++ b/solution.py
@@ -1,8 +1,11 @@
+import functools
 import math
 
 import jax
 import jax.numpy as jnp
 from jax import lax
+from jax.experimental import pallas as pl
+from jax.experimental.pallas import tpu as pltpu
 from jax.sharding import PartitionSpec as P
 
 MOMENTUM_DECAY = 0.9
@@ -57,6 +60,321 @@
     return (leftover, new_weight, values)
 
 
+LANES = 128
+F32, BF16 = jnp.float32, jnp.bfloat16
+
+
+def split_hi_lo(x):
+    hi = x.astype(BF16)
+    return hi, (x - hi.astype(F32)).astype(BF16)
+
+
+def dot(a, b, dims=((1,), (0,))):
+    return lax.dot_general(a, b, (dims, ((), ())), preferred_element_type=F32)
+
+
+def dot3(a_hi, a_lo, b_hi, b_lo, dims=((1,), (0,))):
+    return dot(a_hi, b_hi, dims) + dot(a_hi, b_lo, dims) + dot(a_lo, b_hi, dims)
+
+
+def fill_basis(band_ref, bh, bl):
+    slabs, bands, width = bh.shape
+    length = slabs * width
+    period = 4 * length
+    freq = jnp.broadcast_to(band_ref[...].astype(F32), (LANES, bands)).T.astype(jnp.int32)
+    lane = lax.broadcasted_iota(jnp.int32, (bands, LANES), 1)
+    row_scale = jnp.where(freq == 0, math.sqrt(1.0 / length), math.sqrt(2.0 / length)).astype(F32)
+
+    def angle(steps):
+        centred = ((steps * freq + period // 2) & (period - 1)) - period // 2
+        return centred.astype(F32) * (math.pi / (2 * length))
+
+    fine, coarse = angle(2 * lane + 1), angle(2 * LANES * lane)
+    cos_fine, sin_fine = row_scale * jnp.cos(fine), row_scale * jnp.sin(fine)
+    cos_coarse, sin_coarse = jnp.cos(coarse), jnp.sin(coarse)
+    for at in range(length // LANES):
+        tile = cos_coarse[:, at : at + 1] * cos_fine - sin_coarse[:, at : at + 1] * sin_fine
+        hi, lo = split_hi_lo(tile)
+        a, col = divmod(at * LANES, width)
+        bh[a, :, col : col + LANES] = hi
+        bl[a, :, col : col + LANES] = lo
+
+
+def kernel(
+    n, reps, band_ref, x_hbm, og_hbm, w_hbm, mom_hbm, left_hbm, nw_hbm, val_hbm,
+    x, oc, og, w, mom, bh, bl, perm, xa, grad, left, upd, nw, odd, even, pin, pout, vin, cz, sg, val,
+    load_sem, oc_send, oc_recv, og_send, og_recv, p_send, p_recv, v_send, v_recv,
+    c_send, c_recv, s_send, s_recv, out_sem,
+):
+    me, rep = lax.axis_index("fsdp"), lax.axis_index("rep")
+    tokens, depth = x.shape
+    own_rows, width = w.shape
+    slabs, bands, _ = bh.shape
+    groups = mom.shape[0]
+    scaling = 1.0 / math.sqrt(depth)
+    bits = n.bit_length() - 1
+
+    def peer(k):
+        return sum((((me // 2**b) % 2 + (k >> b) % 2) % 2) * 2**b for b in range(bits))
+
+    def across(d):
+        return lax.rem(rep + d, reps)
+
+    def columns(which):
+        return pl.ds(pl.multiple_of(which * own_rows, LANES), own_rows)
+
+    def to_peer(k, src, dst, send, recv):
+        return pltpu.make_async_remote_copy(
+            src_ref=src, dst_ref=dst, send_sem=send, recv_sem=recv,
+            device_id={"fsdp": peer(k)}, device_id_type=pl.DeviceIdType.MESH,
+        )
+
+    def to_rep(d, src, dst, send, recv):
+        return pltpu.make_async_remote_copy(
+            src_ref=src, dst_ref=dst, send_sem=send, recv_sem=recv,
+            device_id={"rep": across(d)}, device_id_type=pl.DeviceIdType.MESH,
+        )
+
+    loads = [
+        pltpu.make_async_copy(x_hbm.at[0], x, load_sem.at[0]),
+        pltpu.make_async_copy(og_hbm.at[0], og.at[0], load_sem.at[1]),
+        pltpu.make_async_copy(w_hbm, w, load_sem.at[2]),
+        pltpu.make_async_copy(mom_hbm.at[0], mom, load_sem.at[3]),
+        pltpu.make_async_copy(x_hbm.at[0, :, columns(me)], oc.at[0], load_sem.at[4]),
+    ]
+    for load in loads:
+        load.start()
+
+    barrier = pltpu.get_barrier_semaphore()
+    for k in range(1, n):
+        pl.semaphore_signal(
+            barrier, inc=1, device_id={"fsdp": peer(k)}, device_id_type=pl.DeviceIdType.MESH
+        )
+    for d in range(1, reps):
+        pl.semaphore_signal(
+            barrier, inc=1, device_id={"rep": across(d)}, device_id_type=pl.DeviceIdType.MESH
+        )
+    pl.semaphore_wait(barrier, n - 1 + reps - 1)
+
+    og_copies = {}
+    for k in [k for k in range(2, n, 2)] + [1]:
+        og_copies[k] = to_peer(k, og_hbm.at[0], og.at[k], og_send.at[k], og_recv.at[k])
+    oc_copies = {
+        k: to_peer(k, x_hbm.at[0, :, columns(peer(k))], oc.at[k], oc_send.at[k], oc_recv.at[k])
+        for k in range(1, n)
+    }
+    order = sorted(range(2, n), key=lambda k: (-bin(k >> 1).count("1"), k % 2, k))
+    for k in range(2, n, 2):
+        og_copies[k].start()
+    for k in order:
+        oc_copies[k].start()
+    og_copies[1].start()
+    oc_copies[1].start()
+
+    fill_basis(band_ref, bh, bl)
+
+    forward = {
+        k: to_peer(1, og.at[k], og.at[k + 1], og_send.at[k + 1], og_recv.at[k + 1])
+        for k in range(2, n, 2)
+    }
+    loads[0].wait()
+    span = slabs * LANES
+    row = lax.broadcasted_iota(jnp.int32, (span, LANES), 0)
+    lane = lax.broadcasted_iota(jnp.int32, (span, LANES), 1)
+    for a in range(slabs):
+        perm[:, a * LANES : (a + 1) * LANES] = (row == slabs * lane + a).astype(F32).astype(BF16)
+    for piece in range(depth // span):
+        sorted_piece = dot(x[:, piece * span : (piece + 1) * span], perm[...]).astype(BF16)
+        for a in range(slabs):
+            xa[a * tokens : (a + 1) * tokens, piece * LANES : (piece + 1) * LANES] = sorted_piece[
+                :, a * LANES : (a + 1) * LANES
+            ]
+    for k in range(2, n, 2):
+        og_copies[k].wait_recv()
+        forward[k].start()
+
+    for load in loads[1:]:
+        load.wait()
+    tiles = range(width // LANES)
+    first = dot(oc[0], og[0], ((0,), (0,)))
+    for t in tiles:
+        grad[t] = first[:, t * LANES : (t + 1) * LANES]
+    even[0] = dot(oc[0], w[...])
+    to_partner = {}
+    for k in [1] + order:
+        oc_copies[k].wait_recv()
+        if k % 2 and k > 1:
+            forward[k - 1].wait_recv()
+        elif k == 1:
+            og_copies[1].wait_recv()
+        product = dot(oc[k], og[k], ((0,), (0,)))
+        for t in tiles:
+            grad[t] += product[:, t * LANES : (t + 1) * LANES]
+        partial = dot(oc[k], w[...])
+        if k % 2:
+            odd[k // 2] = partial.astype(BF16)
+            to_partner[k] = to_peer(1, odd.at[k // 2], pin.at[k // 2], p_send.at[k // 2], p_recv.at[k // 2])
+            to_partner[k].start()
+        else:
+            even[k // 2] = partial
+
+    total = None
+    for a in range(slabs):
+        rows = [grad[t, pl.ds(a, groups, stride=slabs), :] for t in tiles]
+        part = MOMENTUM_DECAY * mom[:, a * width : (a + 1) * width] + scaling * jnp.concatenate(rows, 1)
+        mom[:, a * width : (a + 1) * width] = part
+        hi, lo = split_hi_lo(part)
+        term = dot3(hi, lo, bh[a], bl[a], ((1,), (1,)))
+        total = term if total is None else total + term
+    cz[rep] = total.astype(BF16)
+    c_copies = [to_rep(d, cz.at[rep], cz.at[rep], c_send.at[d], c_recv.at[d]) for d in range(1, reps)]
+    for c in c_copies:
+        c.start()
+
+    v_copies = []
+    for h in range(1, n // 2):
+        to_partner[2 * h + 1].wait_recv()
+        pout[h] = (even[h] + pin[h].astype(F32)).astype(BF16)
+        copy = to_peer(2 * h, pout.at[h], vin.at[h], v_send.at[h], v_recv.at[h])
+        copy.start()
+        v_copies.append(copy)
+
+    c_hi, c_lo = split_hi_lo(total)
+    for a in range(slabs):
+        cut = slice(a * width, (a + 1) * width)
+        left[:, cut] = mom[:, cut] - dot3(c_hi, c_lo, bh[a], bl[a])
+    out_left = pltpu.make_async_copy(left, left_hbm.at[0], out_sem.at[0])
+    out_left.start()
+
+    for c in c_copies:
+        c.wait_recv()
+    shared = cz[0].astype(F32)
+    for d in range(1, reps):
+        shared = shared + cz[d].astype(F32)
+    shared = shared / reps
+    sg[me] = shared.astype(BF16)
+    s_copies = [to_peer(k, sg.at[me], sg.at[me], s_send.at[k], s_recv.at[k]) for k in range(1, n)]
+    for s in s_copies:
+        s.start()
+
+    s_hi, s_lo = split_hi_lo(shared)
+    for a in range(slabs):
+        product = dot3(s_hi, s_lo, bh[a], bl[a])
+        for t in tiles:
+            upd[t, pl.ds(a, groups, stride=slabs), :] = product[:, t * LANES : (t + 1) * LANES]
+    for t in tiles:
+        cut = slice(t * LANES, (t + 1) * LANES)
+        nw[:, cut] = rebuild_rows(w[:, cut], upd[t])
+    out_nw = pltpu.make_async_copy(nw, nw_hbm, out_sem.at[1])
+    out_nw.start()
+
+    to_partner[1].wait_recv()
+    base = even[0] + pin[0].astype(F32)
+    for h in range(1, n // 2):
+        v_copies[h - 1].wait_recv()
+        base = base + vin[h].astype(F32)
+    for s in s_copies:
+        s.wait_recv()
+    mixed = dot(xa[...], sg[...].reshape(n * groups, bands))
+    change = None
+    for a in range(slabs):
+        hi, lo = split_hi_lo(mixed[a * tokens : (a + 1) * tokens])
+        term = dot3(hi, lo, bh[a], bl[a])
+        change = term if change is None else change + term
+    val[...] = ((base - LEARNING_RATE * change) * scaling).astype(BF16)
+    out_val = pltpu.make_async_copy(val, val_hbm.at[0], out_sem.at[2])
+    out_val.start()
+
+    for k in range(1, n):
+        oc_copies[k].wait_send()
+        if k % 2 and k > 1:
+            forward[k - 1].wait_send()
+        else:
+            og_copies[k].wait_send()
+        if k % 2:
+            to_partner[k].wait_send()
+    for copy in v_copies + c_copies + s_copies:
+        copy.wait_send()
+    out_left.wait()
+    out_nw.wait()
+    out_val.wait()
+
+
+def fused_shards(n, reps, inputs, out_grad, weight, momentum, band_index):
+    tokens, depth = inputs.shape[1:]
+    own_rows, width = weight.shape
+    groups, group_len = momentum.shape[1:]
+    slabs, bands = group_len // width, band_index.shape[0]
+    half = n // 2
+    dma = pltpu.SemaphoreType.DMA
+    span = slabs * LANES
+    anywhere = pl.BlockSpec(memory_space=pl.ANY)
+    return pl.pallas_call(
+        functools.partial(kernel, n, reps),
+        out_shape=(
+            jax.ShapeDtypeStruct(momentum.shape, F32),
+            jax.ShapeDtypeStruct(weight.shape, BF16),
+            jax.ShapeDtypeStruct(out_grad.shape, BF16),
+        ),
+        in_specs=[pl.BlockSpec(memory_space=pltpu.VMEM)] + [anywhere] * 4,
+        out_specs=(anywhere,) * 3,
+        scratch_shapes=[
+            pltpu.VMEM((tokens, depth), BF16),
+            pltpu.VMEM((n, tokens, own_rows), BF16),
+            pltpu.VMEM((n, tokens, width), BF16),
+            pltpu.VMEM((own_rows, width), BF16),
+            pltpu.VMEM((groups, group_len), F32),
+            pltpu.VMEM((slabs, bands, width), BF16),
+            pltpu.VMEM((slabs, bands, width), BF16),
+            pltpu.VMEM((span, span), BF16),
+            pltpu.VMEM((slabs * tokens, depth // slabs), BF16),
+            pltpu.VMEM((width // LANES, own_rows, LANES), F32),
+            pltpu.VMEM((groups, group_len), F32),
+            pltpu.VMEM((width // LANES, own_rows, LANES), F32),
+            pltpu.VMEM((own_rows, width), BF16),
+            pltpu.VMEM((half, tokens, width), BF16),
+            pltpu.VMEM((half, tokens, width), F32),
+            pltpu.VMEM((half, tokens, width), BF16),
+            pltpu.VMEM((half, tokens, width), BF16),
+            pltpu.VMEM((half, tokens, width), BF16),
+            pltpu.VMEM((reps, groups, bands), BF16),
+            pltpu.VMEM((n, groups, bands), BF16),
+            pltpu.VMEM((tokens, width), BF16),
+            dma((5,)),
+            dma((n,)), dma((n,)), dma((n,)), dma((n,)),
+            dma((half,)), dma((half,)), dma((half,)), dma((half,)),
+            dma((reps,)), dma((reps,)), dma((n,)), dma((n,)),
+            dma((3,)),
+        ],
+        compiler_params=pltpu.CompilerParams(collective_id=0, has_side_effects=True),
+    )(band_index.reshape(1, -1), inputs, out_grad, weight, momentum)
+
+
+def fits_kernel(n, inputs, weight, momentum, band_index):
+    tokens, depth = inputs.shape[1:]
+    own_rows, width = weight.shape
+    groups, group_len = momentum.shape[1:]
+    return (
+        n > 1
+        and n & (n - 1) == 0
+        and group_len & (group_len - 1) == 0
+        and tokens % 16 == 0
+        and own_rows % LANES == 0
+        and width % LANES == 0
+        and groups % 16 == 0
+        and group_len % width == 0
+        and group_len // LANES <= LANES
+        and depth % (group_len // width * LANES) == 0
+        and band_index.shape[0] % LANES == 0
+    )
+
+
+def program(n, reps, inputs, out_grad, weight, momentum, band_index):
+    if fits_kernel(n, inputs, weight, momentum, band_index):
+        return fused_shards(n, reps, inputs, out_grad, weight, momentum, band_index)
+    return shards(inputs, out_grad, weight, momentum, band_index)
+
+
 def solution(mesh):
     placed = (
         P("rep", "fsdp", None),
@@ -66,7 +384,7 @@
         P(),
     )
     return jax.shard_map(
-        shards,
+        functools.partial(program, mesh.shape["fsdp"], mesh.shape["rep"]),
         mesh=mesh,
         in_specs=placed,
         out_specs=(P("rep", "fsdp", None), P("fsdp", None), P("rep", "fsdp", None)),

time: 128 us -> 45 us (0.35)
  waiting for transfers between devices: 47.4 us -> 0 us
  Pallas kernels: 0 us -> 40.1 us
  matrix products: 35.6 us -> 0 us
  blocking collectives: 19.2 us -> 0 us
  between operations: 14.1 us -> 0.65 us
  starting transfers between devices: 5.27 us -> 0 us
  other arithmetic: 2.09 us -> 0 us
    pallas_call x0 -> x1, Pallas kernels: none -> 40.1 us  [fused_shards(): pl.pallas_call(functools.partial(kernel, n, reps), out_shape=(jax.ShapeDt...]
    dot_general x5 -> x0, matrix products: 35.6 us -> none  [the longest x1 11 us: shards(): coeffs = jnp.dot(moment, dct_basis.T, precision=highest)]
    all_gather x2 -> x0, waiting for transfers between devices: 30 us -> none  [the longest x1 23.7 us: shards(): lax.all_gather(new_weight, 'fsdp', axis=0, tiled=True)]
    psum x1 -> x0, blocking collectives: 19.2 us -> none  [shards(): shared = lax.psum(coeffs, 'rep') / lax.axis_size('rep')]
    all_to_all x1 -> x0, waiting for transfers between devices: 16.7 us -> none  [shards(): lax.all_to_all(tok_inputs, 'fsdp', split_axis=1, concat_axis=0, tiled=True)]
    all_to_all x1 -> x0, starting transfers between devices: 5.2 us -> none  [shards(): lax.all_to_all(tok_inputs, 'fsdp', split_axis=1, concat_axis=0, tiled=True)]
    convert_element_type x1 -> x0, other arithmetic: 2.08 us -> none  [rebuild_rows(): (old_rows.astype(jnp.float32) - LEARNING_RATE * update_rows).astype(jnp.b...]
    unnamed x8 -> x7, local copies, waits for them, and re-layouts: 3.05 us -> 4.01 us
  transfers between devices with their start and end apart: 3 -> 0, of which waited for: 3 -> 0; matrix products, arithmetic and copies ran while one was open for 10% -> 0% of each run, Pallas kernels for 0% -> 0%
where the time goes in v1:
time: 45 us; the launch traced here: 44.8 us
  Pallas kernels  40.1 us (89%)
  local copies, waits for them, and re-layouts  4.01 us (9%)
  between operations  0.65 us (1%)
    pallas_call x1, Pallas kernels, fused_shards(): pl.pallas_call(functools.partial(kernel, n, reps), out_shape=(jax.ShapeDt...  40.1 us
    unnamed x7, local copies, waits for them, and re-layouts  4.01 us

profile of v1, /device:TPU:0, one launch (start us, length us, event | category | flops | bytes accessed | tf_op | source)
XLA Modules:
  0.0 44.8 jit_solution(9152454560122006056)
XLA Ops:
  0.6 40.1 %shard_map.76 = (f32[1,64,4096]{2,1,0:T(8,128)}, bf16[512,512]{1,0:T(8,128)(2,1)}, bf16[1,128,512]{2,1,0:T(8,128)(2,1)}) custom-call(s32[1,128]{1,0:T(1,128)} %bitcast.1, bf16[1,128,4096]{2,1,0:T(8,128)(2,1)} %x_hbm.1, bf16[1,128,512]{2,1,0:T(8,128)(2,1)} %og_hbm.1, bf16[512,512]{1,0:T(8,128)(2,1)} %w_hbm.1, f32[1,64,4096]{2,1,0:T(8,128)} %mom_hbm.1), custom_call_target="tpu_custom_call" | custom-call | tf_op jit(solution)/shard_map/pallas_call | solution.py:312
  40.8 0.0 copy-start
  40.8 2.3 %copy.11 = f32[1,64,4096]{2,1,0:T(8,128)} copy(f32[1,64,4096]{2,1,0:T(8,128)} %get-tuple-element.6) | data formatting | bytes 2097152
  43.1 0.0 copy-done
  43.1 0.0 copy-start.1
  43.1 0.8 %copy.12 = bf16[512,512]{1,0:T(8,128)(2,1)} copy(bf16[512,512]{1,0:T(8,128)(2,1)S(1)} %copy-done) | data formatting | bytes 1048576
  43.9 0.2 copy-done.1
  44.1 0.7 %copy.13 = bf16[1,128,512]{2,1,0:T(8,128)(2,1)} copy(bf16[1,128,512]{2,1,0:T(8,128)(2,1)S(1)} %copy-done.1) | data formatting | bytes 262144
Async XLA Ops:
  40.8 2.3 %copy-start = (bf16[512,512]{1,0:T(8,128)(2,1)S(1)}, bf16[512,512]{1,0:T(8,128)(2,1)}, u32[]{:S(2)}) copy-start(bf16[512,512]{1,0:T(8,128)(2,1)} %get-tuple-element.7) | copy-start | bytes 1572868
  43.1 1.0 %copy-start.1 = (bf16[1,128,512]{2,1,0:T(8,128)(2,1)S(1)}, bf16[1,128,512]{2,1,0:T(8,128)(2,1)}, u32[]{:S(2)}) copy-start(bf16[1,128,512]{2,1,0:T(8,128)(2,1)} %get-tuple-element.8) | copy-start | bytes 393220

commit v2 on v1

--- a/solution.py
+++ b/solution.py
@@ -77,7 +77,7 @@
     return dot(a_hi, b_hi, dims) + dot(a_hi, b_lo, dims) + dot(a_lo, b_hi, dims)
 
 
-def fill_basis(band_ref, bh, bl):
+def fill_basis(band_ref, bh, bl, bt):
     slabs, bands, width = bh.shape
     length = slabs * width
     period = 4 * length
@@ -98,13 +98,16 @@
         a, col = divmod(at * LANES, width)
         bh[a, :, col : col + LANES] = hi
         bl[a, :, col : col + LANES] = lo
+        hi, lo = split_hi_lo(tile.T)
+        bt[at * LANES : (at + 1) * LANES, :bands] = hi
+        bt[at * LANES : (at + 1) * LANES, bands:] = lo
 
 
 def kernel(
-    n, reps, band_ref, x_hbm, og_hbm, w_hbm, mom_hbm, left_hbm, nw_hbm, val_hbm,
-    x, oc, og, w, mom, bh, bl, perm, xa, grad, left, upd, nw, odd, even, pin, pout, vin, cz, sg, val,
+    n, reps, band_ref, x_hbm, og_hbm, w_hbm, mom_hbm, left, nw, val,
+    x, oc, og, w, mom, bh, bl, bt, perm, xa, grad, upd, odd, even, pin, pout, vin, cz, sg,
     load_sem, oc_send, oc_recv, og_send, og_recv, p_send, p_recv, v_send, v_recv,
-    c_send, c_recv, s_send, s_recv, out_sem,
+    c_send, c_recv, s_send, s_recv,
 ):
     me, rep = lax.axis_index("fsdp"), lax.axis_index("rep")
     tokens, depth = x.shape
@@ -171,7 +174,7 @@
     og_copies[1].start()
     oc_copies[1].start()
 
-    fill_basis(band_ref, bh, bl)
+    fill_basis(band_ref, bh, bl, bt)
 
     forward = {
         k: to_peer(1, og.at[k], og.at[k + 1], og_send.at[k + 1], og_recv.at[k + 1])
@@ -218,19 +221,6 @@
         else:
             even[k // 2] = partial
 
-    total = None
-    for a in range(slabs):
-        rows = [grad[t, pl.ds(a, groups, stride=slabs), :] for t in tiles]
-        part = MOMENTUM_DECAY * mom[:, a * width : (a + 1) * width] + scaling * jnp.concatenate(rows, 1)
-        mom[:, a * width : (a + 1) * width] = part
-        hi, lo = split_hi_lo(part)
-        term = dot3(hi, lo, bh[a], bl[a], ((1,), (1,)))
-        total = term if total is None else total + term
-    cz[rep] = total.astype(BF16)
-    c_copies = [to_rep(d, cz.at[rep], cz.at[rep], c_send.at[d], c_recv.at[d]) for d in range(1, reps)]
-    for c in c_copies:
-        c.start()
-
     v_copies = []
     for h in range(1, n // 2):
         to_partner[2 * h + 1].wait_recv()
@@ -239,12 +229,26 @@
         copy.start()
         v_copies.append(copy)
 
+    wide, narrow = None, None
+    for a in range(slabs):
+        rows = [grad[t, pl.ds(a, groups, stride=slabs), :] for t in tiles]
+        part = MOMENTUM_DECAY * mom[:, a * width : (a + 1) * width] + scaling * jnp.concatenate(rows, 1)
+        mom[:, a * width : (a + 1) * width] = part
+        hi, lo = split_hi_lo(part)
+        both = dot(hi, bt[a * width : (a + 1) * width, :])
+        rest = dot(lo, bt[a * width : (a + 1) * width, :bands])
+        wide = both if wide is None else wide + both
+        narrow = rest if narrow is None else narrow + rest
+    total = wide[:, :bands] + (wide[:, bands:] + narrow)
+    cz[rep] = total.astype(BF16)
+    c_copies = [to_rep(d, cz.at[rep], cz.at[rep], c_send.at[d], c_recv.at[d]) for d in range(1, reps)]
+    for c in c_copies:
+        c.start()
+
     c_hi, c_lo = split_hi_lo(total)
     for a in range(slabs):
         cut = slice(a * width, (a + 1) * width)
-        left[:, cut] = mom[:, cut] - dot3(c_hi, c_lo, bh[a], bl[a])
-    out_left = pltpu.make_async_copy(left, left_hbm.at[0], out_sem.at[0])
-    out_left.start()
+        left[0, :, cut] = mom[:, cut] - dot3(c_hi, c_lo, bh[a], bl[a])
 
     for c in c_copies:
         c.wait_recv()
@@ -265,8 +269,6 @@
     for t in tiles:
         cut = slice(t * LANES, (t + 1) * LANES)
         nw[:, cut] = rebuild_rows(w[:, cut], upd[t])
-    out_nw = pltpu.make_async_copy(nw, nw_hbm, out_sem.at[1])
-    out_nw.start()
 
     to_partner[1].wait_recv()
     base = even[0] + pin[0].astype(F32)
@@ -276,14 +278,10 @@
     for s in s_copies:
         s.wait_recv()
     mixed = dot(xa[...], sg[...].reshape(n * groups, bands))
-    change = None
-    for a in range(slabs):
-        hi, lo = split_hi_lo(mixed[a * tokens : (a + 1) * tokens])
-        term = dot3(hi, lo, bh[a], bl[a])
-        change = term if change is None else change + term
-    val[...] = ((base - LEARNING_RATE * change) * scaling).astype(BF16)
-    out_val = pltpu.make_async_copy(val, val_hbm.at[0], out_sem.at[2])
-    out_val.start()
+    mixed = jnp.concatenate([mixed[a * tokens : (a + 1) * tokens] for a in range(slabs)], 1)
+    hi, lo = split_hi_lo(mixed)
+    change = dot3(hi, lo, bh[...].reshape(slabs * bands, width), bl[...].reshape(slabs * bands, width))
+    val[0] = ((base - LEARNING_RATE * change) * scaling).astype(BF16)
 
     for k in range(1, n):
         oc_copies[k].wait_send()
@@ -295,9 +293,6 @@
             to_partner[k].wait_send()
     for copy in v_copies + c_copies + s_copies:
         copy.wait_send()
-    out_left.wait()
-    out_nw.wait()
-    out_val.wait()
 
 
 def fused_shards(n, reps, inputs, out_grad, weight, momentum, band_index):
@@ -312,12 +307,12 @@
     return pl.pallas_call(
         functools.partial(kernel, n, reps),
         out_shape=(
-            jax.ShapeDtypeStruct(momentum.shape, F32),
-            jax.ShapeDtypeStruct(weight.shape, BF16),
-            jax.ShapeDtypeStruct(out_grad.shape, BF16),
+            pltpu.VMEM(momentum.shape, F32),
+            pltpu.VMEM(weight.shape, BF16),
+            pltpu.VMEM(out_grad.shape, BF16),
         ),
         in_specs=[pl.BlockSpec(memory_space=pltpu.VMEM)] + [anywhere] * 4,
-        out_specs=(anywhere,) * 3,
+        out_specs=(pl.BlockSpec(memory_space=pltpu.VMEM),) * 3,
         scratch_shapes=[
             pltpu.VMEM((tokens, depth), BF16),
             pltpu.VMEM((n, tokens, own_rows), BF16),
@@ -326,12 +321,11 @@
             pltpu.VMEM((groups, group_len), F32),
             pltpu.VMEM((slabs, bands, width), BF16),
             pltpu.VMEM((slabs, bands, width), BF16),
+            pltpu.VMEM((group_len, 2 * bands), BF16),
             pltpu.VMEM((span, span), BF16),
             pltpu.VMEM((slabs * tokens, depth // slabs), BF16),
             pltpu.VMEM((width // LANES, own_rows, LANES), F32),
-            pltpu.VMEM((groups, group_len), F32),
             pltpu.VMEM((width // LANES, own_rows, LANES), F32),
-            pltpu.VMEM((own_rows, width), BF16),
             pltpu.VMEM((half, tokens, width), BF16),
             pltpu.VMEM((half, tokens, width), F32),
             pltpu.VMEM((half, tokens, width), BF16),
@@ -339,12 +333,10 @@
             pltpu.VMEM((half, tokens, width), BF16),
             pltpu.VMEM((reps, groups, bands), BF16),
             pltpu.VMEM((n, groups, bands), BF16),
-            pltpu.VMEM((tokens, width), BF16),
             dma((5,)),
             dma((n,)), dma((n,)), dma((n,)), dma((n,)),
             dma((half,)), dma((half,)), dma((half,)), dma((half,)),
             dma((reps,)), dma((reps,)), dma((n,)), dma((n,)),
-            dma((3,)),
         ],
         compiler_params=pltpu.CompilerParams(collective_id=0, has_side_effects=True),
     )(band_index.reshape(1, -1), inputs, out_grad, weight, momentum)

time: 45 us -> 40.7 us (0.904)
  Pallas kernels: 40.1 us -> 37.5 us
  local copies, waits for them, and re-layouts: 4.01 us -> 2.42 us
    pallas_call x1, Pallas kernels: 40.1 us -> 37.5 us  [fused_shards(): pl.pallas_call(functools.partial(kernel, n, reps), out_shape=(pltpu.VMEM(...]
    unnamed x7 -> x3, local copies, waits for them, and re-layouts: 4.01 us -> 2.42 us
where the time goes in v2:
time: 40.7 us; the launch traced here: 40.5 us
  Pallas kernels  37.5 us (92%)
  local copies, waits for them, and re-layouts  2.42 us (6%)
  between operations  0.64 us (2%)
    pallas_call x1, Pallas kernels, fused_shards(): pl.pallas_call(functools.partial(kernel, n, reps), out_shape=(pltpu.VMEM(...  37.5 us
    unnamed x3, local copies, waits for them, and re-layouts  2.42 us

profile of v2, /device:TPU:0, one launch (start us, length us, event | category | flops | bytes accessed | tf_op | source)
XLA Modules:
  0.0 40.5 jit_solution(4468465114127193986)
XLA Ops:
  0.6 37.5 %shard_map.76 = (f32[1,64,4096]{2,1,0:T(8,128)S(1)}, bf16[512,512]{1,0:T(8,128)(2,1)S(1)}, bf16[1,128,512]{2,1,0:T(8,128)(2,1)S(1)}) custom-call(s32[1,128]{1,0:T(1,128)} %bitcast.1, bf16[1,128,4096]{2,1,0:T(8,128)(2,1)} %x_hbm.1, bf16[1,128,512]{2,1,0:T(8,128)(2,1)} %og_hbm.1, bf16[512,512]{1,0:T(8,128)(2,1)} %w_hbm.1, f32[1,64,4096]{2,1,0:T(8,128)} %mom_hbm.1), custom_call_target="tpu_custom_call" | custom-call | tf_op jit(solution)/shard_map/pallas_call | solution.py:307
  38.1 1.0 %copy.11 = f32[1,64,4096]{2,1,0:T(8,128)} copy(f32[1,64,4096]{2,1,0:T(8,128)S(1)} %get-tuple-element.3) | data formatting | bytes 2097152
  39.1 0.7 %copy.13 = bf16[1,128,512]{2,1,0:T(8,128)(2,1)} copy(bf16[1,128,512]{2,1,0:T(8,128)(2,1)S(1)} %get-tuple-element.5) | data formatting | bytes 262144
  39.7 0.8 %copy.12 = bf16[512,512]{1,0:T(8,128)(2,1)} copy(bf16[512,512]{1,0:T(8,128)(2,1)S(1)} %get-tuple-element.4) | data formatting | bytes 1048576

commit v3 on v2

--- a/solution.py
+++ b/solution.py
@@ -106,7 +106,7 @@
 def kernel(
     n, reps, band_ref, x_hbm, og_hbm, w_hbm, mom_hbm, left, nw, val,
     x, oc, og, w, mom, bh, bl, bt, perm, xa, grad, upd, odd, even, pin, pout, vin, cz, sg,
-    load_sem, oc_send, oc_recv, og_send, og_recv, p_send, p_recv, v_send, v_recv,
+    load_sem, oc_send, oc_recv, og_send, og_recv, r_send, r_recv, p_send, p_recv, v_send, v_recv,
     c_send, c_recv, s_send, s_recv,
 ):
     me, rep = lax.axis_index("fsdp"), lax.axis_index("rep")
@@ -149,37 +149,59 @@
         load.start()
 
     barrier = pltpu.get_barrier_semaphore()
-    for k in range(1, n):
-        pl.semaphore_signal(
-            barrier, inc=1, device_id={"fsdp": peer(k)}, device_id_type=pl.DeviceIdType.MESH
-        )
     for d in range(1, reps):
         pl.semaphore_signal(
             barrier, inc=1, device_id={"rep": across(d)}, device_id_type=pl.DeviceIdType.MESH
         )
+    for k in range(n - 1, 0, -1):
+        pl.semaphore_signal(
+            barrier, inc=1, device_id={"fsdp": peer(k)}, device_id_type=pl.DeviceIdType.MESH
+        )
     pl.semaphore_wait(barrier, n - 1 + reps - 1)
 
-    og_copies = {}
-    for k in [k for k in range(2, n, 2)] + [1]:
-        og_copies[k] = to_peer(k, og_hbm.at[0], og.at[k], og_send.at[k], og_recv.at[k])
+    def crossings(k):
+        return bin(k >> 1).count("1")
+
+    relayed = [k for k in range(2, n, 2) if crossings(k) == 2]
+    direct = [k for k in range(2, n, 2) if k not in relayed]
+    order = sorted(range(2, n), key=lambda k: (-crossings(k), k % 2, k))
+    og_copies = {
+        k: to_peer(k, og_hbm.at[0], og.at[k], og_send.at[k], og_recv.at[k]) for k in direct + [1]
+    }
     oc_copies = {
         k: to_peer(k, x_hbm.at[0, :, columns(peer(k))], oc.at[k], oc_send.at[k], oc_recv.at[k])
         for k in range(1, n)
     }
-    order = sorted(range(2, n), key=lambda k: (-bin(k >> 1).count("1"), k % 2, k))
-    for k in range(2, n, 2):
-        og_copies[k].start()
-    for k in order:
-        oc_copies[k].start()
-    og_copies[1].start()
-    oc_copies[1].start()
-
-    fill_basis(band_ref, bh, bl, bt)
-
     forward = {
         k: to_peer(1, og.at[k], og.at[k + 1], og_send.at[k + 1], og_recv.at[k + 1])
         for k in range(2, n, 2)
     }
+    relays = {}
+    for k in relayed:
+        low = k & -k
+        for side, via in enumerate((low, k - low)):
+            part = pl.ds(side * (tokens // 2), tokens // 2)
+            relays[k, side] = to_peer(
+                via, og.at[k - via, part], og.at[k, part], r_send.at[k, side], r_recv.at[k, side]
+            )
+    for copy in og_copies.values():
+        copy.start()
+    early = [k for k in order if crossings(k) > 1] + [1]
+    for k in early:
+        oc_copies[k].start()
+
+    fill_basis(band_ref, bh, bl, bt)
+
+    for k in direct:
+        og_copies[k].wait_recv()
+    for copy in relays.values():
+        copy.start()
+    for k in order:
+        if k not in early:
+            oc_copies[k].start()
+    for k in direct:
+        forward[k].start()
+
     loads[0].wait()
     span = slabs * LANES
     row = lax.broadcasted_iota(jnp.int32, (span, LANES), 0)
@@ -192,8 +214,9 @@
             xa[a * tokens : (a + 1) * tokens, piece * LANES : (piece + 1) * LANES] = sorted_piece[
                 :, a * LANES : (a + 1) * LANES
             ]
-    for k in range(2, n, 2):
-        og_copies[k].wait_recv()
+    for k in relayed:
+        relays[k, 0].wait_recv()
+        relays[k, 1].wait_recv()
         forward[k].start()
 
     for load in loads[1:]:
@@ -287,12 +310,26 @@
         oc_copies[k].wait_send()
         if k % 2 and k > 1:
             forward[k - 1].wait_send()
+        elif k in relayed:
+            relays[k, 0].wait_send()
+            relays[k, 1].wait_send()
         else:
             og_copies[k].wait_send()
         if k % 2:
             to_partner[k].wait_send()
     for copy in v_copies + c_copies + s_copies:
         copy.wait_send()
+
+
+def store_kernel(left, nw, val, left_hbm, nw_hbm, val_hbm, sems):
+    copies = [
+        pltpu.make_async_copy(src, dst, sems.at[i])
+        for i, (src, dst) in enumerate(((left, left_hbm), (nw, nw_hbm), (val, val_hbm)))
+    ]
+    for copy in copies:
+        copy.start()
+    for copy in copies:
+        copy.wait()
 
 
 def fused_shards(n, reps, inputs, out_grad, weight, momentum, band_index):
@@ -304,7 +341,7 @@
     dma = pltpu.SemaphoreType.DMA
     span = slabs * LANES
     anywhere = pl.BlockSpec(memory_space=pl.ANY)
-    return pl.pallas_call(
+    held = pl.pallas_call(
         functools.partial(kernel, n, reps),
         out_shape=(
             pltpu.VMEM(momentum.shape, F32),
@@ -334,12 +371,20 @@
             pltpu.VMEM((reps, groups, bands), BF16),
             pltpu.VMEM((n, groups, bands), BF16),
             dma((5,)),
-            dma((n,)), dma((n,)), dma((n,)), dma((n,)),
+            dma((n,)), dma((n,)), dma((n,)), dma((n,)), dma((n, 2)), dma((n, 2)),
             dma((half,)), dma((half,)), dma((half,)), dma((half,)),
             dma((reps,)), dma((reps,)), dma((n,)), dma((n,)),
         ],
         compiler_params=pltpu.CompilerParams(collective_id=0, has_side_effects=True),
     )(band_index.reshape(1, -1), inputs, out_grad, weight, momentum)
+    return pl.pallas_call(
+        store_kernel,
+        out_shape=tuple(jax.ShapeDtypeStruct(a.shape, a.dtype) for a in held),
+        in_specs=[anywhere] * 3,
+        out_specs=(anywhere,) * 3,
+        scratch_shapes=[dma((3,))],
+        compiler_params=pltpu.CompilerParams(vmem_limit_bytes=1 << 20),
+    )(*held)
 
 
 def fits_kernel(n, inputs, weight, momentum, band_index):
@@ -350,7 +395,7 @@
         n > 1
         and n & (n - 1) == 0
         and group_len & (group_len - 1) == 0
-        and tokens % 16 == 0
+        and tokens % 32 == 0
         and own_rows % LANES == 0
         and width % LANES == 0
         and groups % 16 == 0

time: 40.7 us -> 38.4 us (0.943)
  local copies, waits for them, and re-layouts: 2.42 us -> 0 us
    unnamed x3 -> x0, local copies, waits for them, and re-layouts: 2.42 us -> none
    pallas_call x0 -> x1, Pallas kernels: none -> 1.2 us  [fused_shards(): pl.pallas_call(store_kernel, out_shape=tuple((jax.ShapeDtypeStruct(a.shap...]
    pallas_call x1, Pallas kernels: 37.5 us -> 36.4 us  [fused_shards(): pl.pallas_call(functools.partial(kernel, n, reps), out_shape=(pltpu.VMEM(...]
where the time goes in v3:
time: 38.4 us; the launch traced here: 38.2 us
  Pallas kernels  37.6 us (98%)
  between operations  0.64 us (2%)
    pallas_call x1, Pallas kernels, fused_shards(): pl.pallas_call(functools.partial(kernel, n, reps), out_shape=(pltpu.VMEM(...  36.4 us
    pallas_call x1, Pallas kernels, fused_shards(): pl.pallas_call(store_kernel, out_shape=tuple((jax.ShapeDtypeStruct(a.shap...  1.2 us

profile of v3, /device:TPU:0, one launch (start us, length us, event | category | flops | bytes accessed | tf_op | source)
XLA Modules:
  0.0 38.2 jit_solution(11276865175222835802)
XLA Ops:
  0.6 36.4 %shard_map.76 = (f32[1,64,4096]{2,1,0:T(8,128)S(1)}, bf16[512,512]{1,0:T(8,128)(2,1)S(1)}, bf16[1,128,512]{2,1,0:T(8,128)(2,1)S(1)}) custom-call(s32[1,128]{1,0:T(1,128)} %bitcast.1, bf16[1,128,4096]{2,1,0:T(8,128)(2,1)} %x_hbm.1, bf16[1,128,512]{2,1,0:T(8,128)(2,1)} %og_hbm.1, bf16[512,512]{1,0:T(8,128)(2,1)} %w_hbm.1, f32[1,64,4096]{2,1,0:T(8,128)} %mom_hbm.1), custom_call_target="tpu_custom_call" | custom-call | tf_op jit(solution)/shard_map/pallas_call | solution.py:344
  37.0 1.2 %shard_map.77 = (f32[1,64,4096]{2,1,0:T(8,128)}, bf16[512,512]{1,0:T(8,128)(2,1)}, bf16[1,128,512]{2,1,0:T(8,128)(2,1)}) custom-call(f32[1,64,4096]{2,1,0:T(8,128)S(1)} %get-tuple-element.6.left, bf16[512,512]{1,0:T(8,128)(2,1)S(1)} %get-tuple-element.7.nw, bf16[1,128,512]{2,1,0:T(8,128)(2,1)S(1)} %get-tuple-element.8.val), custom_call_target="tpu_custom_call" | custom-call | tf_op jit(solution)/shard_map/pallas_call | solution.py:380

commit v4 on v3

--- a/solution.py
+++ b/solution.py
@@ -164,7 +164,7 @@
 
     relayed = [k for k in range(2, n, 2) if crossings(k) == 2]
     direct = [k for k in range(2, n, 2) if k not in relayed]
-    order = sorted(range(2, n), key=lambda k: (-crossings(k), k % 2, k))
+    order = sorted(range(2, n), key=lambda k: (-crossings(k), 1 - k % 2, k))
     og_copies = {
         k: to_peer(k, og_hbm.at[0], og.at[k], og_send.at[k], og_recv.at[k]) for k in direct + [1]
     }
@@ -244,13 +244,13 @@
         else:
             even[k // 2] = partial
 
-    v_copies = []
-    for h in range(1, n // 2):
+    v_copies = {}
+    for h in range(n // 2 - 1, 0, -1):
         to_partner[2 * h + 1].wait_recv()
         pout[h] = (even[h] + pin[h].astype(F32)).astype(BF16)
         copy = to_peer(2 * h, pout.at[h], vin.at[h], v_send.at[h], v_recv.at[h])
         copy.start()
-        v_copies.append(copy)
+        v_copies[h] = copy
 
     wide, narrow = None, None
     for a in range(slabs):
@@ -280,7 +280,7 @@
         shared = shared + cz[d].astype(F32)
     shared = shared / reps
     sg[me] = shared.astype(BF16)
-    s_copies = [to_peer(k, sg.at[me], sg.at[me], s_send.at[k], s_recv.at[k]) for k in range(1, n)]
+    s_copies = [to_peer(k, sg.at[me], sg.at[me], s_send.at[k], s_recv.at[k]) for k in range(n - 1, 0, -1)]
     for s in s_copies:
         s.start()
 
@@ -296,7 +296,7 @@
     to_partner[1].wait_recv()
     base = even[0] + pin[0].astype(F32)
     for h in range(1, n // 2):
-        v_copies[h - 1].wait_recv()
+        v_copies[h].wait_recv()
         base = base + vin[h].astype(F32)
     for s in s_copies:
         s.wait_recv()
@@ -317,7 +317,7 @@
             og_copies[k].wait_send()
         if k % 2:
             to_partner[k].wait_send()
-    for copy in v_copies + c_copies + s_copies:
+    for copy in list(v_copies.values()) + c_copies + s_copies:
         copy.wait_send()
 
 

time: 38.4 us -> 37.7 us (0.982)
  Pallas kernels: 37.6 us -> 36.9 us
    pallas_call x1, Pallas kernels: 36.4 us -> 35.7 us  [fused_shards(): pl.pallas_call(functools.partial(kernel, n, reps), out_shape=(pltpu.VMEM(...]
where the time goes in v4:
time: 37.7 us; the launch traced here: 37.6 us
  Pallas kernels  36.9 us (98%)
  between operations  0.64 us (2%)
    pallas_call x1, Pallas kernels, fused_shards(): pl.pallas_call(functools.partial(kernel, n, reps), out_shape=(pltpu.VMEM(...  35.7 us
    pallas_call x1, Pallas kernels, fused_shards(): pl.pallas_call(store_kernel, out_shape=tuple((jax.ShapeDtypeStruct(a.shap...  1.2 us

profile of v4, /device:TPU:0, one launch (start us, length us, event | category | flops | bytes accessed | tf_op | source)
XLA Modules:
  0.0 37.6 jit_solution(13199146799306955150)
XLA Ops:
  0.6 35.7 %shard_map.76 = (f32[1,64,4096]{2,1,0:T(8,128)S(1)}, bf16[512,512]{1,0:T(8,128)(2,1)S(1)}, bf16[1,128,512]{2,1,0:T(8,128)(2,1)S(1)}) custom-call(s32[1,128]{1,0:T(1,128)} %bitcast.1, bf16[1,128,4096]{2,1,0:T(8,128)(2,1)} %x_hbm.1, bf16[1,128,512]{2,1,0:T(8,128)(2,1)} %og_hbm.1, bf16[512,512]{1,0:T(8,128)(2,1)} %w_hbm.1, f32[1,64,4096]{2,1,0:T(8,128)} %mom_hbm.1), custom_call_target="tpu_custom_call" | custom-call | tf_op jit(solution)/shard_map/pallas_call | solution.py:344
  36.4 1.2 %shard_map.77 = (f32[1,64,4096]{2,1,0:T(8,128)}, bf16[512,512]{1,0:T(8,128)(2,1)}, bf16[1,128,512]{2,1,0:T(8,128)(2,1)}) custom-call(f32[1,64,4096]{2,1,0:T(8,128)S(1)} %get-tuple-element.6.left, bf16[512,512]{1,0:T(8,128)(2,1)S(1)} %get-tuple-element.7.nw, bf16[1,128,512]{2,1,0:T(8,128)(2,1)S(1)} %get-tuple-element.8.val), custom_call_target="tpu_custom_call" | custom-call | tf_op jit(solution)/shard_map/pallas_call | solution.py:380
